TPU v7x, 512 devices: a whole 4x8x8 slice. The times are simulated.
512 devices in a mesh: dp: 16 (over y_lo, z), gx: 8 (over x, core), gy: 4 (over y_hi).
Axes of the slice: x: 4, y: 8 (y_hi: 4, y_lo: 2; y = y_hi * 2 + y_lo), z: 8, core: 2. Of those that a mesh axis runs over, the one named last changes fastest.
Arguments:
- fields: bfloat16 [16, 20, 32, 16384], P('dp', None, None, ('gx', 'gy')), may hold values from -6 to 6
- cotangent: bfloat16 [16, 20, 32, 16384], P('dp', None, None, ('gx', 'gy')), may hold values from -6 to 6
- mix_weight: bfloat16 [20, 20], replicated, may hold values from -1.25 to 1.25
- spectral_weight: bfloat16 [288, 2, 20, 20], P(('gx', 'gy')), may hold values from -1 to 1
Outputs:
- output: bfloat16 [16, 20, 32, 16384], P('dp', None, None, ('gx', 'gy'))
- spectral_grad: float32 [288, 2, 20, 20], P(('gx', 'gy'))
- mixing_grad: float32 [20, 20], replicated
All inputs are finite; a program needn't handle non-finite values.
Results may differ from a plain program's by a relative error of at most 0.0031.
Values may be sent and summed in bfloat16 or wider, within the bound.
A program may use at most 64 MiB of HBM per device.

v0:
```python
import math
import jax
import jax.numpy as jnp
from jax import lax
from jax.sharding import PartitionSpec as P

NX = 128
NY = 128
KX = 24
KY = 12
P_SIZE = 32
MODES = 288
HI = lax.Precision.HIGHEST


def gelu_value(h):
    k = math.sqrt(2.0 / math.pi)
    t = jnp.tanh(k * (h + 0.044715 * h * h * h))
    return 0.5 * h * (1.0 + t)


def gelu_slope(h):
    k = math.sqrt(2.0 / math.pi)
    t = jnp.tanh(k * (h + 0.044715 * h * h * h))
    return 0.5 * (1.0 + t) + 0.5 * h * (1.0 - t * t) * k * (1.0 + 3.0 * 0.044715 * h * h)


def axis_table(waves, n):
    cells = jnp.arange(n, dtype=jnp.int32)
    angle = 2.0 * math.pi / n * (waves[:, None] * cells[None, :] % n).astype(jnp.float32)
    return (jnp.cos(angle), jnp.sin(angle))


def tables():
    index = jnp.arange(KX, dtype=jnp.int32)
    waves_x = jnp.where(index < KX // 2, index, NX - KX + index)
    cos_x, sin_x = axis_table(waves_x, NX)
    cos_y, sin_y = axis_table(jnp.arange(KY, dtype=jnp.int32), NY)
    return (cos_x, sin_x, cos_y, sin_y)


def forward_dft(data, scale):
    cos_x, sin_x, cos_y, sin_y = tables()
    a_re = jnp.einsum("cpxy,ky->cpxk", data, cos_y, precision=HI)
    a_im = -jnp.einsum("cpxy,ky->cpxk", data, sin_y, precision=HI)
    s_re = jnp.einsum("cpxk,jx->jkcp", a_re, cos_x, precision=HI) + jnp.einsum(
        "cpxk,jx->jkcp", a_im, sin_x, precision=HI
    )
    s_im = jnp.einsum("cpxk,jx->jkcp", a_im, cos_x, precision=HI) - jnp.einsum(
        "cpxk,jx->jkcp", a_re, sin_x, precision=HI
    )
    chans, planes = (data.shape[0], data.shape[1])
    return scale * jnp.stack(
        [s_re.reshape(MODES, chans, planes), s_im.reshape(MODES, chans, planes)], axis=1
    )


def inverse_dft(vals, scale):
    cos_x, sin_x, cos_y, sin_y = tables()
    chans, planes = (vals.shape[2], vals.shape[3])
    v_re = vals[:, 0].reshape(KX, KY, chans, planes)
    v_im = vals[:, 1].reshape(KX, KY, chans, planes)
    b_re = jnp.einsum("jkdp,jx->dpxk", v_re, cos_x, precision=HI) - jnp.einsum(
        "jkdp,jx->dpxk", v_im, sin_x, precision=HI
    )
    b_im = jnp.einsum("jkdp,jx->dpxk", v_re, sin_x, precision=HI) + jnp.einsum(
        "jkdp,jx->dpxk", v_im, cos_x, precision=HI
    )
    return scale * (
        jnp.einsum("dpxk,ky->dpxy", b_re, cos_y, precision=HI)
        - jnp.einsum("dpxk,ky->dpxy", b_im, sin_y, precision=HI)
    )


def spectral_mix(spec, weight):
    w = weight.astype(jnp.float32)
    v_re = jnp.einsum("mcp,mcd->mdp", spec[:, 0], w[:, 0], precision=HI) - jnp.einsum(
        "mcp,mcd->mdp", spec[:, 1], w[:, 1], precision=HI
    )
    v_im = jnp.einsum("mcp,mcd->mdp", spec[:, 0], w[:, 1], precision=HI) + jnp.einsum(
        "mcp,mcd->mdp", spec[:, 1], w[:, 0], precision=HI
    )
    return jnp.stack([v_re, v_im], axis=1)


def grads_of(spec, gspec):
    g_re = jnp.einsum("mcp,mdp->mcd", spec[:, 0], gspec[:, 0], precision=HI) + jnp.einsum(
        "mcp,mdp->mcd", spec[:, 1], gspec[:, 1], precision=HI
    )
    g_im = jnp.einsum("mcp,mdp->mcd", spec[:, 0], gspec[:, 1], precision=HI) - jnp.einsum(
        "mcp,mdp->mcd", spec[:, 1], gspec[:, 0], precision=HI
    )
    return jnp.stack([g_re, g_im], axis=1)


def to_planes(block):
    chans, planes, rows_x, full_y = block.shape
    size_x = lax.axis_size("gx")
    size_y = lax.axis_size("gy")
    moved = lax.all_to_all(
        lax.all_to_all(block, "gx", split_axis=1, concat_axis=2, tiled=True),
        "gy",
        split_axis=1,
        concat_axis=2,
        tiled=True,
    )
    own = moved.shape[1]
    moved = moved.reshape(chans, own, size_y, size_x, rows_x, full_y)
    moved = jnp.transpose(moved, (0, 1, 3, 2, 4, 5))
    return moved.reshape(chans, own, size_x * size_y * rows_x, full_y)


def to_cells(plane_block):
    chans, own, full_x, full_y = plane_block.shape
    size_x = lax.axis_size("gx")
    size_y = lax.axis_size("gy")
    rows_x = full_x // (size_x * size_y)
    moved = lax.all_to_all(
        lax.all_to_all(plane_block, "gx", split_axis=2, concat_axis=1, tiled=True),
        "gy",
        split_axis=2,
        concat_axis=1,
        tiled=True,
    )
    moved = moved.reshape(chans, size_y, size_x, own, rows_x, full_y)
    moved = jnp.transpose(moved, (0, 2, 1, 3, 4, 5))
    return moved.reshape(chans, size_x * size_y * own, rows_x, full_y)


def local(fields, cotangent, mix_weight, spectral_weight):
    flat = fields[0]
    grad_out = cotangent[0].astype(jnp.float32)
    chans, planes, cells = flat.shape
    rows_x = cells // NY
    norm_in = 1.0 / math.sqrt(NX * NY)
    norm_out = 1.0 / math.sqrt(MODES)
    samples = lax.axis_size("dp")
    mixed = jnp.einsum("cpq,cd->dpq", flat, mix_weight, preferred_element_type=jnp.float32)
    plane_field = to_planes(flat.reshape(chans, planes, rows_x, NY)).astype(jnp.float32)
    spec = forward_dft(plane_field, norm_in)
    full_weight = lax.all_gather(spectral_weight, ("gx", "gy"), axis=0, tiled=True)
    vals = spectral_mix(spec, full_weight)
    branch = to_cells(inverse_dft(vals, norm_out)).reshape(chans, planes, cells)
    pre = branch + mixed
    output = gelu_value(pre).astype(jnp.bfloat16).reshape(1, chans, planes, cells)
    back = (grad_out * gelu_slope(pre)).astype(jnp.bfloat16)
    local_mix = jnp.einsum("cpq,dpq->cd", flat, back, preferred_element_type=jnp.float32)
    mix_scale = 1.0 / math.sqrt(samples * P_SIZE * NX * NY)
    spec_scale = 1.0 / math.sqrt(samples * P_SIZE)
    plane_back = to_planes(back.reshape(chans, planes, rows_x, NY)).astype(jnp.float32)
    gspec = forward_dft(plane_back, norm_out)
    local_spec = grads_of(spec, gspec)
    share = lax.psum_scatter(local_spec, ("gx", "gy"), scatter_dimension=0, tiled=True)
    spectral_grad = lax.psum(share, "dp") * spec_scale
    mixing_grad = lax.psum(local_mix, ("dp", "gx", "gy")) * mix_scale
    return (output, spectral_grad, mixing_grad)


def solution(mesh):
    return jax.shard_map(
        local,
        mesh=mesh,
        in_specs=(
            P("dp", None, None, ("gx", "gy")),
            P("dp", None, None, ("gx", "gy")),
            P(),
            P(("gx", "gy"), None, None, None),
        ),
        out_specs=(P("dp", None, None, ("gx", "gy")), P(("gx", "gy"), None, None, None), P()),
        check_vma=False,
    )
```

profile of v0, /device:TPU:2, one launch (start us, length us, event | category | flops | bytes accessed | tf_op | source)
XLA Modules:
  0.0 713.6 jit_solution(4944024013968660867)
XLA Ops:
  7.2 1.6 reshape_squeeze.3
  8.8 1.1 copy.251
  9.9 10.0 %all-to-all-start = ((bf16[20,32,4,128]{3,2,0,1:T(4,128)(2,1)}), bf16[20,32,4,128]{3,2,0,1:T(4,128)(2,1)}, u32[]{:S(2)}, u32[]{:S(2)}) async-start(bf16[20,32,4,128]{3,2,0,1:T(4,128)(2,1)} %copy.251), calls=%async_computation | async-start | bytes 1310720 | tf_op jit(solution)/shard_map/all_to_all | solution.py:101
  19.9 112.9 %all_gather.3 = bf16[288,2,20,20]{3,1,2,0:T(2,128)(2,1)S(1)} all-gather(bf16[9,2,20,20]{3,1,2,0:T(2,128)(2,1)S(1)} %copy-done.5), channel_id=1, replica_groups=mesh['dp'=16,'gx'=8,'gy'=4] {'gx','gy'}, dimensions={0}, use_global_device_ids=true | all-gather | bytes 475200 | tf_op jit(solution)/shard_map/all_gather | solution.py:141
  132.7 1.3 copy.252
  135.2 4.8 all-to-all-start.1
  140.1 5.6 fusion.165
  145.7 6.4 copy.317
  152.1 4.7 copy.318
  156.8 1.9 all-to-all-done.1
  158.7 1.2 copy.255
  168.9 2.2 fusion.24
  171.1 2.2 fusion.8
  173.3 1.3 copy.271
  174.7 20.8 %all_to_all.81 = f32[20,1,128,128]{3,1,0,2:T(1,128)S(1)} all-to-all(f32[20,1,128,128]{3,1,0,2:T(1,128)S(1)} %copy.271), channel_id=1, replica_groups=mesh['dp'=16,'gx'=8,'gy'=4] {'gx'}, dimensions={2} | all-to-all | bytes 2621440 | tf_op jit(solution)/shard_map/all_to_all | solution.py:119
  196.1 39.4 %all_to_all.82 = f32[20,8,16,128]{3,1,0,2:T(8,128)S(1)} all-to-all(f32[20,8,16,128]{3,1,0,2:T(8,128)S(1)} %copy.273), channel_id=1, replica_groups=mesh['dp'=16,'gx'=8,'gy'=4] {'gy'}, dimensions={2} | all-to-all | bytes 2621440 | tf_op jit(solution)/shard_map/all_to_all | solution.py:118
  237.4 4.7 fusion.6
  242.4 14.0 %all_to_all.83 = bf16[20,32,4,128]{3,2,0,1:T(4,128)(2,1)S(1)} all-to-all(bf16[20,32,4,128]{3,2,0,1:T(4,128)(2,1)S(1)} %reshape.261), channel_id=1, replica_groups=mesh['dp'=16,'gx'=8,'gy'=4] {'gx'}, dimensions={1} | all-to-all | bytes 1310720 | tf_op jit(solution)/shard_map/all_to_all | solution.py:101
  256.8 22.2 %all_to_all.84 = bf16[20,4,32,128]{3,2,0,1:T(8,128)(2,1)S(1)} all-to-all(bf16[20,4,32,128]{3,2,0,1:T(8,128)(2,1)S(1)} %copy.282), channel_id=1, replica_groups=mesh['dp'=16,'gx'=8,'gy'=4] {'gy'}, dimensions={1} | all-to-all | bytes 1310720 | tf_op jit(solution)/shard_map/all_to_all | solution.py:100
  285.7 6.0 copy.290
  291.8 1.3 dynamic-slice
  295.5 107.2 %psum.15 = f32[20,20]{0,1:T(8,128)S(1)} all-reduce(f32[20,20]{0,1:T(8,128)S(1)} %convolution_bitcast_fusion.1), channel_id=1, replica_groups=mesh['dp'=16,'gx'=8,'gy'=4] {'dp','gx','gy'}, use_global_device_ids=true, to_apply=%region_2.3 | all-reduce | flops 400 | bytes 3200 | tf_op jit(solution)/shard_map/psum | solution.py:155
  403.4 233.1 %all-reduce.3.cloned.1.call-done = f32[288,2,20,20]{3,1,2,0:T(2,128)} async-done(((f32[288,2,20,20]{3,1,2,0:T(2,128)}), f32[288,2,20,20]{3,1,2,0:T(2,128)}) %all-reduce.3.cloned.1.call-update) | async-done | bytes 921616
  637.4 68.6 %psum.14 = f32[9,2,20,20]{3,1,2,0:T(2,128)S(1)} all-reduce(f32[9,2,20,20]{3,1,2,0:T(2,128)S(1)} %constant_dynamic-slice_fusion), channel_id=1, replica_groups=mesh['dp'=16,'gx'=8,'gy'=4] {'dp'}, use_global_device_ids=true, to_apply=%region_1.2 | all-reduce | flops 7200 | bytes 57600 | tf_op jit(solution)/shard_map/psum | solution.py:154
  (74 shorter events, 24.1 us)
Async XLA Ops:
  7.2 229.7 %copy-start = (bf16[20,20]{1,0:T(8,128)(2,1)S(1)}, bf16[20,20]{1,0:T(8,128)(2,1)}, u32[]{:S(2)}) copy-start(bf16[20,20]{1,0:T(8,128)(2,1)} %param.6) | copy-start | bytes 2404
  8.8 11.0 %copy-start.5 = (bf16[9,2,20,20]{3,1,2,0:T(2,128)(2,1)S(1)}, bf16[9,2,20,20]{3,1,2,0:T(2,128)(2,1)}, u32[]{:S(2)}) copy-start(bf16[9,2,20,20]{3,1,2,0:T(2,128)(2,1)} %param.7) | copy-start | bytes 43204
  9.9 122.8 %all-to-all-start = ((bf16[20,32,4,128]{3,2,0,1:T(4,128)(2,1)}), bf16[20,32,4,128]{3,2,0,1:T(4,128)(2,1)}, u32[]{:S(2)}, u32[]{:S(2)}) async-start(bf16[20,32,4,128]{3,2,0,1:T(4,128)(2,1)} %copy.251), calls=%async_computation | async-start | bytes 1310720 | tf_op jit(solution)/shard_map/all_to_all | solution.py:101
  135.2 23.4 %all-to-all-start.1 = ((bf16[20,4,32,128]{3,2,0,1:T(8,128)(2,1)}), bf16[20,4,32,128]{3,2,0,1:T(8,128)(2,1)}, u32[]{:S(2)}, u32[]{:S(2)}) async-start(bf16[20,4,32,128]{3,2,0,1:T(8,128)(2,1)} %copy.254), calls=%async_computation.1 | async-start | bytes 1310720 | tf_op jit(solution)/shard_map/all_to_all | solution.py:100
  140.1 496.3 %all-reduce.3.cloned.1.call-start = ((), (), s32[]{:S(2)}) async-start(), calls=%async_computation.6 | async-start | bytes 11796480
  145.7 6.4 copy-start.1
  161.4 4.8 copy-start.2
  236.3 1.1 copy-start.4
  291.8 2.0 copy-start.3
Sparse Core Ops, SparseCore 0:
  291.9 344.4 all-reduce.2
where the time goes:
time: 714 us
  blocking collectives  385 us (54%)
  waiting for transfers between devices  235 us (33%)
  local copies, waits for them, and re-layouts  40.8 us (6%)
  matrix products  21.4 us (3%)
  between operations  15.1 us (2%)
  starting transfers between devices  14.8 us (2%)
    unnamed x2, waiting for transfers between devices  233 us
    all_gather x1, blocking collectives, local(): lax.all_gather(spectral_weight, ('gx', 'gy'), axis=0, tiled=True)  113 us
    psum x1, blocking collectives, local(): mixing_grad = lax.psum(local_mix, ('dp', 'gx', 'gy')) * mix_scale  107 us
    psum x1, blocking collectives, local(): spectral_grad = lax.psum(share, 'dp') * spec_scale  68.6 us
    all_to_all x1, blocking collectives, to_cells(): lax.all_to_all(lax.all_to_all(plane_block, 'gx', split_axis=2, concat_axi...  39.4 us
    all_to_all x1, blocking collectives, to_planes(): lax.all_to_all(lax.all_to_all(block, 'gx', split_axis=1, concat_axis=2, t...  22.2 us
    all_to_all x1, blocking collectives, to_cells(): lax.all_to_all(plane_block, 'gx', split_axis=2, concat_axis=1, tiled=True)  20.8 us
    unnamed x21, local copies, waits for them, and re-layouts  15.6 us
  transfers between devices with their start and end apart: 3, of which 2 were waited for; matrix products, arithmetic and copies ran while one was open for 3% of the time, Pallas kernels for 0%

commit v1 on v0

--- a/solution.py
+++ b/solution.py
@@ -11,6 +11,13 @@
 P_SIZE = 32
 MODES = 288
 HI = lax.Precision.HIGHEST
+
+
+def swapped_in(x, mesh_axis, along):
+    size = lax.axis_size(mesh_axis)
+    blocks = jnp.stack([x for _ in range(size)])
+    blocks = lax.all_to_all(blocks, mesh_axis, split_axis=0, concat_axis=0)
+    return jnp.concatenate(blocks, axis=along)
 
 
 def gelu_value(h):
@@ -138,7 +145,7 @@
     mixed = jnp.einsum("cpq,cd->dpq", flat, mix_weight, preferred_element_type=jnp.float32)
     plane_field = to_planes(flat.reshape(chans, planes, rows_x, NY)).astype(jnp.float32)
     spec = forward_dft(plane_field, norm_in)
-    full_weight = lax.all_gather(spectral_weight, ("gx", "gy"), axis=0, tiled=True)
+    full_weight = swapped_in(spectral_weight, ("gx", "gy"), 0)
     vals = spectral_mix(spec, full_weight)
     branch = to_cells(inverse_dft(vals, norm_out)).reshape(chans, planes, cells)
     pre = branch + mixed

time: 714 us -> 637 us (0.89)
  blocking collectives: 385 us -> 276 us
  waiting for transfers between devices: 235 us -> 253 us
  local copies, waits for them, and re-layouts: 40.8 us -> 50.4 us
    all_gather x1 -> x0, blocking collectives: 113 us -> none  [local(): lax.all_gather(spectral_weight, ('gx', 'gy'), axis=0, tiled=True)]
    all_to_all x0 -> x1, waiting for transfers between devices: none -> 13.5 us  [swapped_in(): blocks = lax.all_to_all(blocks, mesh_axis, split_axis=0, concat_axis=0)]
    unnamed x21 -> x22, local copies, waits for them, and re-layouts: 15.6 us -> 14.1 us
  transfers between devices with their start and end apart: 3 -> 4, of which waited for: 2 -> 3; matrix products, arithmetic and copies ran while one was open for 3% -> 5% of each run, Pallas kernels for 0% -> 0%
where the time goes in v1:
time: 637 us
  blocking collectives  276 us (43%)
  waiting for transfers between devices  253 us (40%)
  local copies, waits for them, and re-layouts  50.4 us (8%)
  matrix products  21.4 us (3%)
  starting transfers between devices  19.2 us (3%)
  between operations  15.1 us (2%)
    unnamed x2, waiting for transfers between devices  235 us
    psum x1, blocking collectives, local(): mixing_grad = lax.psum(local_mix, ('dp', 'gx', 'gy')) * mix_scale  113 us
    psum x1, blocking collectives, local(): spectral_grad = lax.psum(share, 'dp') * spec_scale  68.6 us
    all_to_all x1, blocking collectives, to_cells(): lax.all_to_all(lax.all_to_all(plane_block, 'gx', split_axis=2, concat_axi...  37.5 us
    all_to_all x1, blocking collectives, to_planes(): lax.all_to_all(lax.all_to_all(block, 'gx', split_axis=1, concat_axis=2, t...  21.8 us
    all_to_all x1, blocking collectives, to_cells(): lax.all_to_all(plane_block, 'gx', split_axis=2, concat_axis=1, tiled=True)  21.5 us
    unnamed x22, local copies, waits for them, and re-layouts  14.1 us
    all_to_all x1, blocking collectives, to_planes(): lax.all_to_all(block, 'gx', split_axis=1, concat_axis=2, tiled=True)  14.1 us
  transfers between devices with their start and end apart: 4, of which 3 were waited for; matrix products, arithmetic and copies ran while one was open for 5% of the time, Pallas kernels for 0%

profile of v1, /device:TPU:2, one launch (start us, length us, event | category | flops | bytes accessed | tf_op | source)
XLA Modules:
  0.0 636.5 jit_solution(11557925213219354697)
XLA Ops:
  7.2 1.7 reshape_squeeze.3
  9.9 10.0 %all-to-all-start = ((bf16[20,32,4,128]{3,2,0,1:T(4,128)(2,1)}), bf16[20,32,4,128]{3,2,0,1:T(4,128)(2,1)}, u32[]{:S(2)}, u32[]{:S(2)}) async-start(bf16[20,32,4,128]{3,2,0,1:T(4,128)(2,1)} %copy.335), calls=%async_computation | async-start | bytes 1310720 | tf_op jit(solution)/shard_map/all_to_all | solution.py:108
  19.9 1.5 broadcast_bitcast_fusion
  21.4 4.4 reshape.269
  25.8 4.5 all-to-all-done
  30.3 5.0 all-to-all-start.2
  37.8 13.5 %all-to-all-done.2 = bf16[32,2,3600]{2,1,0:T(2,128)(2,1)S(1)} async-done(((bf16[32,2,3600]{2,1,0:T(2,128)(2,1)}), bf16[32,2,3600]{2,1,0:T(2,128)(2,1)S(1)}, u32[]{:S(2)}, u32[]{:S(2)}) %all-to-all-start.2) | async-done | bytes 460832 | tf_op jit(solution)/shard_map/all_to_all | solution.py:19
  51.3 4.2 all-to-all-start.1
  55.6 3.6 reshape.270
  59.2 5.7 fusion.165
  64.9 6.4 %copy.347 = bf16[288,1,20,20]{0,3,2,1:T(8,128)(2,1)S(1)} copy(bf16[288,1,20,20]{3,1,2,0:T(2,128)(2,1)} %get-tuple-element.39) | data formatting | bytes 460800 | tf_op jit(solution)/shard_map/slice | solution.py:84
  71.3 4.7 copy.348
  86.1 2.2 fusion.24
  88.4 2.2 fusion.8
  90.6 1.3 copy.355
  92.0 21.5 %all_to_all.86 = f32[20,1,128,128]{3,1,0,2:T(1,128)S(1)} all-to-all(f32[20,1,128,128]{3,1,0,2:T(1,128)S(1)} %copy.355), channel_id=1, replica_groups=mesh['dp'=16,'gx'=8,'gy'=4] {'gx'}, dimensions={2} | all-to-all | bytes 2621440 | tf_op jit(solution)/shard_map/all_to_all | solution.py:126
  114.0 37.5 %all_to_all.87 = f32[20,8,16,128]{3,1,0,2:T(8,128)S(1)} all-to-all(f32[20,8,16,128]{3,1,0,2:T(8,128)S(1)} %copy.357), channel_id=1, replica_groups=mesh['dp'=16,'gx'=8,'gy'=4] {'gy'}, dimensions={2} | all-to-all | bytes 2621440 | tf_op jit(solution)/shard_map/all_to_all | solution.py:125
  153.5 4.7 fusion.6
  158.5 14.1 %all_to_all.88 = bf16[20,32,4,128]{3,2,0,1:T(4,128)(2,1)S(1)} all-to-all(bf16[20,32,4,128]{3,2,0,1:T(4,128)(2,1)S(1)} %reshape.267), channel_id=1, replica_groups=mesh['dp'=16,'gx'=8,'gy'=4] {'gx'}, dimensions={1} | all-to-all | bytes 1310720 | tf_op jit(solution)/shard_map/all_to_all | solution.py:108
  172.9 21.8 %all_to_all.89 = bf16[20,4,32,128]{3,2,0,1:T(8,128)(2,1)S(1)} all-to-all(bf16[20,4,32,128]{3,2,0,1:T(8,128)(2,1)S(1)} %copy.366), channel_id=1, replica_groups=mesh['dp'=16,'gx'=8,'gy'=4] {'gy'}, dimensions={1} | all-to-all | bytes 1310720 | tf_op jit(solution)/shard_map/all_to_all | solution.py:107
  201.4 6.0 copy.374
  211.2 113.0 %psum.15 = f32[20,20]{0,1:T(8,128)S(1)} all-reduce(f32[20,20]{0,1:T(8,128)S(1)} %convolution_bitcast_fusion.1), channel_id=1, replica_groups=mesh['dp'=16,'gx'=8,'gy'=4] {'dp','gx','gy'}, use_global_device_ids=true, to_apply=%region_2.3 | all-reduce | flops 400 | bytes 3200 | tf_op jit(solution)/shard_map/psum | solution.py:162
  324.8 234.5 %all-reduce.3.cloned.1.call-done = f32[288,2,20,20]{3,1,2,0:T(2,128)} async-done(((f32[288,2,20,20]{3,1,2,0:T(2,128)}), f32[288,2,20,20]{3,1,2,0:T(2,128)}) %all-reduce.3.cloned.1.call-update) | async-done | bytes 921616
  560.3 68.6 %psum.14 = f32[9,2,20,20]{3,1,2,0:T(2,128)S(1)} all-reduce(f32[9,2,20,20]{3,1,2,0:T(2,128)S(1)} %constant_dynamic-slice_fusion), channel_id=1, replica_groups=mesh['dp'=16,'gx'=8,'gy'=4] {'dp'}, use_global_device_ids=true, to_apply=%region_1.2 | all-reduce | flops 7200 | bytes 57600 | tf_op jit(solution)/shard_map/psum | solution.py:161
  (78 shorter events, 28.9 us)
Async XLA Ops:
  7.2 12.7 %copy-start = (bf16[9,2,20,20]{3,1,2,0:T(2,128)(2,1)S(1)}, bf16[9,2,20,20]{3,1,2,0:T(2,128)(2,1)}, u32[]{:S(2)}) copy-start(bf16[9,2,20,20]{3,1,2,0:T(2,128)(2,1)} %param.7) | copy-start | bytes 43204
  9.9 20.4 %all-to-all-start = ((bf16[20,32,4,128]{3,2,0,1:T(4,128)(2,1)}), bf16[20,32,4,128]{3,2,0,1:T(4,128)(2,1)}, u32[]{:S(2)}, u32[]{:S(2)}) async-start(bf16[20,32,4,128]{3,2,0,1:T(4,128)(2,1)} %copy.335), calls=%async_computation | async-start | bytes 1310720 | tf_op jit(solution)/shard_map/all_to_all | solution.py:108
  30.3 21.0 %all-to-all-start.2 = ((bf16[32,2,3600]{2,1,0:T(2,128)(2,1)}), bf16[32,2,3600]{2,1,0:T(2,128)(2,1)S(1)}, u32[]{:S(2)}, u32[]{:S(2)}) async-start(bf16[32,2,3600]{2,1,0:T(2,128)(2,1)} %reshape.269), calls=%async_computation.2 | async-start | bytes 950272 | tf_op jit(solution)/shard_map/all_to_all | solution.py:19
  51.3 24.6 %all-to-all-start.1 = ((bf16[20,4,32,128]{3,2,0,1:T(8,128)(2,1)}), bf16[20,4,32,128]{3,2,0,1:T(8,128)(2,1)}, u32[]{:S(2)}, u32[]{:S(2)}) async-start(bf16[20,4,32,128]{3,2,0,1:T(8,128)(2,1)} %copy.338), calls=%async_computation.1 | async-start | bytes 1310720 | tf_op jit(solution)/shard_map/all_to_all | solution.py:107
  55.5 503.9 %all-reduce.3.cloned.1.call-start = ((), (), s32[]{:S(2)}) async-start(), calls=%async_computation.7 | async-start | bytes 11796480
  64.9 6.4 %copy-start.1 = (bf16[288,1,20,20]{3,1,2,0:T(2,128)(2,1)S(1)}, bf16[288,1,20,20]{3,1,2,0:T(2,128)(2,1)}, u32[]{:S(2)}) copy-start(bf16[288,1,20,20]{3,1,2,0:T(2,128)(2,1)} %get-tuple-element.40) | copy-start | bytes 691204
  78.7 4.8 copy-start.2
  152.4 1.1 copy-start.4
  152.4 1.1 copy-start.5
  207.4 2.0 copy-start.3
Sparse Core Ops, SparseCore 0:
  207.6 351.7 all-reduce.2
